TPU v7x, 32 devices: a whole 2x2x4 slice. The times are simulated.
32 devices in a mesh: blk: 8 (over z, x), head: 4 (over y, core).
Axes of the slice: x: 2, y: 2, z: 4, core: 2. Of those that a mesh axis runs over, the one named last changes fastest.
Arguments:
- queries: bfloat16 [4096, 1024], P(('blk', 'head')), may hold values from -6 to 6
- key_vectors: bfloat16 [4096, 1024], P(('blk', 'head')), may hold values from -6 to 6
- value_vectors: bfloat16 [4096, 1024], P(('blk', 'head')), may hold values from -6 to 6
- grad_output: bfloat16 [4096, 1024], P(('blk', 'head')), may hold values from -6 to 6
- lengths: int32 [4], replicated, may hold values from 1 to 2048, 4096 in all
Outputs:
- grad_queries: bfloat16 [4096, 1024], P(('blk', 'head'))
- grad_keys: bfloat16 [4096, 1024], P(('blk', 'head'))
- grad_values: bfloat16 [4096, 1024], P(('blk', 'head'))
Inputs may be any that keep to these rules, and one draw needn't show every extreme that they name: 4 positive lengths that sum to 4096; the longest is exactly 2048.
All inputs are finite; a program needn't handle non-finite values.
Results may differ from a plain program's by a relative error of at most 0.0086.
Values may be sent and summed in bfloat16 or wider, within the bound.
No kernel may reach another device: no remote copies, remote signals or barrier semaphores. Data moves between devices by JAX's collectives and lax.ppermute only.
A program may use at most 64 MiB of HBM per device.

v0:
```python
import jax
import jax.numpy as jnp
from jax import lax
from jax.sharding import PartitionSpec as P

DH = 64
WIN = 64


def with_halo(block, sides, width):
    for axis, dim in sides:
        count = lax.axis_size(axis)
        forward = [(i, i + 1) for i in range(count - 1)]
        backward = [(target, source) for source, target in forward]
        low = lax.ppermute(
            lax.slice_in_dim(block, block.shape[dim] - width, None, axis=dim), axis, forward
        )
        high = lax.ppermute(lax.slice_in_dim(block, 0, width, axis=dim), axis, backward)
        block = jnp.concatenate([low, block, high], axis=dim)
    return block


def shifted(block, axis, distance):
    devices = range(lax.axis_size(axis))
    route = [(i - distance, i) for i in devices if i - distance in devices]
    return lax.ppermute(block, axis, route)


def recording_of(positions, rec_ends):
    return jnp.sum((rec_ends[None, :] <= positions[:, None]).astype(jnp.int32), axis=1)


def band_grads(query_rows, grad_rows, key_value, query_first, key_first, rec_ends, frames):
    row_count = query_rows.shape[0]
    columns = query_rows.shape[1]
    head_count = columns // DH
    step_rows = min(512, 2 * WIN)
    key_span = step_rows + 2 * WIN
    score_scale = DH ** (-0.5)
    pair_grad = jnp.zeros((key_value.shape[0], 2 * columns), jnp.float32)
    query_parts = []
    for first_row in range(0, row_count, step_rows):
        query_block = query_rows[first_row : first_row + step_rows].reshape(
            step_rows, head_count, DH
        )
        grad_block = grad_rows[first_row : first_row + step_rows].reshape(step_rows, head_count, DH)
        pair_block = key_value[first_row : first_row + key_span]
        key_block = pair_block[:, :columns].reshape(key_span, head_count, DH)
        value_block = pair_block[:, columns:].reshape(key_span, head_count, DH)
        query_pos = query_first + first_row + jnp.arange(step_rows, dtype=jnp.int32)
        key_pos = key_first + first_row + jnp.arange(key_span, dtype=jnp.int32)
        inside = (key_pos >= 0) & (key_pos < frames)
        visible = jnp.abs(query_pos[:, None] - key_pos[None, :]) <= WIN
        visible = visible & (
            recording_of(query_pos, rec_ends)[:, None] == recording_of(key_pos, rec_ends)[None, :]
        )
        visible = visible & (inside[None, :] | (query_pos[:, None] == key_pos[None, :]))
        scores = (
            jnp.einsum("qhd,khd->hqk", query_block, key_block, preferred_element_type=jnp.float32)
            * score_scale
        )
        scores = jnp.where(visible[None], scores, -1e30)
        row_max = jnp.max(scores, axis=-1, keepdims=True)
        weights = jnp.where(visible[None], jnp.exp(scores - row_max), 0.0)
        probs = weights / jnp.sum(weights, axis=-1, keepdims=True)
        probs_low = probs.astype(jnp.bfloat16)
        value_part = jnp.einsum(
            "hqk,qhd->khd", probs_low, grad_block, preferred_element_type=jnp.float32
        )
        prob_grad = jnp.einsum(
            "qhd,khd->hqk", grad_block, value_block, preferred_element_type=jnp.float32
        )
        row_delta = jnp.sum(probs * prob_grad, axis=-1, keepdims=True)
        score_grad = (probs * (prob_grad - row_delta) * score_scale).astype(jnp.bfloat16)
        query_grad = jnp.einsum(
            "hqk,khd->qhd", score_grad, key_block, preferred_element_type=jnp.float32
        )
        key_part = jnp.einsum(
            "hqk,qhd->khd", score_grad, query_block, preferred_element_type=jnp.float32
        )
        both_parts = jnp.concatenate(
            [key_part.reshape(key_span, columns), value_part.reshape(key_span, columns)], axis=1
        )
        pair_grad = pair_grad.at[first_row : first_row + key_span].add(both_parts)
        query_parts.append(query_grad.reshape(step_rows, columns))
    return (jnp.concatenate(query_parts, axis=0), pair_grad)


def body(queries, key_vectors, value_vectors, grad_output, lengths):
    group_size = lax.axis_size("head")
    block_rows = queries.shape[0] * group_size
    columns = queries.shape[1] // group_size
    frames = block_rows * lax.axis_size("blk")
    head_queries, head_keys, head_values, head_grads = (
        lax.all_to_all(queries, "head", split_axis=1, concat_axis=0, tiled=True),
        lax.all_to_all(key_vectors, "head", split_axis=1, concat_axis=0, tiled=True),
        lax.all_to_all(value_vectors, "head", split_axis=1, concat_axis=0, tiled=True),
        lax.all_to_all(grad_output, "head", split_axis=1, concat_axis=0, tiled=True),
    )
    key_value = jnp.concatenate([head_keys, head_values], axis=1)
    rec_ends = jnp.cumsum(lengths)
    base_pos = lax.axis_index("blk") * block_rows
    extended = with_halo(key_value, (("blk", 0),), WIN)
    query_grad, pair_grad = band_grads(
        head_queries, head_grads, extended, base_pos, base_pos - WIN, rec_ends, frames
    )
    own_rows = pair_grad[WIN : WIN + block_rows]
    arrived = []
    for step_by, rim_rows in ((1, pair_grad[WIN + block_rows :]), (-1, pair_grad[:WIN])):
        arrived.append(shifted(rim_rows, "blk", step_by))
    own_rows = own_rows.at[:WIN].add(arrived[0]).at[block_rows - WIN :].add(arrived[1])
    outputs = (
        lax.all_to_all(
            query_grad.astype(jnp.bfloat16), "head", split_axis=0, concat_axis=1, tiled=True
        ),
        lax.all_to_all(
            own_rows[:, :columns].astype(jnp.bfloat16),
            "head",
            split_axis=0,
            concat_axis=1,
            tiled=True,
        ),
        lax.all_to_all(
            own_rows[:, columns:].astype(jnp.bfloat16),
            "head",
            split_axis=0,
            concat_axis=1,
            tiled=True,
        ),
    )
    return (outputs[0], outputs[1], outputs[2])


def solution(mesh):
    return jax.shard_map(
        body,
        mesh=mesh,
        in_specs=(
            P(("blk", "head"), None),
            P(("blk", "head"), None),
            P(("blk", "head"), None),
            P(("blk", "head"), None),
            P(),
        ),
        out_specs=(P(("blk", "head"), None), P(("blk", "head"), None), P(("blk", "head"), None)),
        check_vma=False,
    )
```

profile of v0, /device:TPU:26, one launch (start us, length us, event | category | flops | bytes accessed | tf_op | source)
XLA Modules:
  0.0 104.3 jit_solution(3987964290970095193)
XLA Ops:
  0.7 1.2 %copy.101 = bf16[128,1024]{0,1:T(8,128)(2,1)S(1)} copy(bf16[128,1024]{1,0:T(8,128)(2,1)} %param.18) | data formatting | bytes 524288 | tf_op args[1]
  2.7 3.4 %all-to-all-start = ((bf16[128,4,256]{2,0,1:T(8,128)(2,1)}), bf16[128,4,256]{2,0,1:T(8,128)(2,1)S(1)}, u32[]{:S(2)}, u32[]{:S(2)}) async-start(bf16[128,4,256]{2,0,1:T(8,128)(2,1)} %copy.102), calls=%async_computation | async-start | bytes 524288 | tf_op jit(solution)/shard_map/all_to_all | solution.py:96
  9.4 2.7 %all-to-all-done = bf16[128,4,256]{2,0,1:T(8,128)(2,1)S(1)} async-done(((bf16[128,4,256]{2,0,1:T(8,128)(2,1)}), bf16[128,4,256]{2,0,1:T(8,128)(2,1)S(1)}, u32[]{:S(2)}, u32[]{:S(2)}) %all-to-all-start) | async-done | bytes 262176 | tf_op jit(solution)/shard_map/all_to_all | solution.py:96
  12.1 3.4 %all-to-all-start.1 = ((bf16[128,4,256]{2,0,1:T(8,128)(2,1)}), bf16[128,4,256]{2,0,1:T(8,128)(2,1)S(1)}, u32[]{:S(2)}, u32[]{:S(2)}) async-start(bf16[128,4,256]{2,0,1:T(8,128)(2,1)} %copy.104), calls=%async_computation.1 | async-start | bytes 524288 | tf_op jit(solution)/shard_map/all_to_all | solution.py:97
  16.3 5.2 %all-to-all-done.1 = bf16[128,4,256]{2,0,1:T(8,128)(2,1)S(1)} async-done(((bf16[128,4,256]{2,0,1:T(8,128)(2,1)}), bf16[128,4,256]{2,0,1:T(8,128)(2,1)S(1)}, u32[]{:S(2)}, u32[]{:S(2)}) %all-to-all-start.1) | async-done | bytes 262176 | tf_op jit(solution)/shard_map/all_to_all | solution.py:97
  21.5 3.4 %all-to-all-start.2 = ((bf16[128,4,256]{0,2,1:T(8,128)(2,1)}), bf16[128,4,256]{0,2,1:T(8,128)(2,1)S(1)}, u32[]{:S(2)}, u32[]{:S(2)}) async-start(bf16[128,4,256]{0,2,1:T(8,128)(2,1)} %bitcast.9), calls=%async_computation.2 | async-start | bytes 524288 | tf_op jit(solution)/shard_map/all_to_all | solution.py:95
  26.4 1.3 %collective-permute-start = (bf16[64,512]{0,1:T(8,128)(2,1)S(1)}, bf16[64,512]{0,1:T(8,128)(2,1)S(1)}, u32[]{:S(2)}, u32[]{:S(2)}) collective-permute-start(bf16[64,512]{0,1:T(8,128)(2,1)S(1)} %get-tuple-element.101), channel_id=1, source_target_pairs={{0,4},{4,8},{8,12},{12,16},{16,20},{20,24},{24,28},{1,5},{5,9},{9,... | collective-permute-start | bytes 196616 | tf_op jit(solution)/shard_map/ppermute | solution.py:15
  27.7 4.6 %collective-permute-start.1 = (bf16[64,512]{0,1:T(8,128)(2,1)S(1)}, bf16[64,512]{0,1:T(8,128)(2,1)S(1)}, u32[]{:S(2)}, u32[]{:S(2)}) collective-permute-start(bf16[64,512]{0,1:T(8,128)(2,1)S(1)} %get-tuple-element.102), channel_id=1, source_target_pairs={{4,0},{8,4},{12,8},{16,12},{20,16},{24,20},{28,24},{5,1},{9,5},{13... | collective-permute-start | bytes 196616 | tf_op jit(solution)/shard_map/ppermute | solution.py:18
  32.2 3.4 %all-to-all-start.3 = ((bf16[128,4,256]{0,2,1:T(8,128)(2,1)}), bf16[128,4,256]{0,2,1:T(8,128)(2,1)S(1)}, u32[]{:S(2)}, u32[]{:S(2)}) async-start(bf16[128,4,256]{0,2,1:T(8,128)(2,1)} %bitcast.14), calls=%async_computation.3 | async-start | bytes 524288 | tf_op jit(solution)/shard_map/all_to_all | solution.py:98
  35.7 6.0 %all-to-all-done.3 = bf16[128,4,256]{0,2,1:T(8,128)(2,1)S(1)} async-done(((bf16[128,4,256]{0,2,1:T(8,128)(2,1)}), bf16[128,4,256]{0,2,1:T(8,128)(2,1)S(1)}, u32[]{:S(2)}, u32[]{:S(2)}) %all-to-all-start.3) | async-done | bytes 262176 | tf_op jit(solution)/shard_map/all_to_all | solution.py:98
  43.0 0.9 convolution_convert_fusion.3
  45.4 0.9 convolution_convert_fusion.2
  46.4 1.0 fusion.45
  47.4 1.3 %fusion.64 = f32[4,256,64]{1,2,0:T(8,128)} fusion(bf16[128,4,64]{0,2,1:T(8,128)(2,1)S(1)} %bitcast.172, f32[4,128]{1,0:T(4,128)S(1)} %get-tuple-element.115, pred[128,256]{0,1:T(8,128)(4,1)S(1)} %fusion.84, bf16[256,4,64]{0,2,1:T(8,128)(2,1)S(1)} %bitcast.183, bf16[128,4,64]{0,2,1:T(8,128)(2,1)S(1)} %bitcast.197), kind=kOutput, calls=%fused_computation.78 | convolution fusion | flops 34341632 | bytes 559104 | tf_op jit(solution)/shard_map/hqk,qhd->khd/dot_general | solution.py:67
  48.9 1.2 %fusion.121 = (f32[4,128]{1,0:T(4,128)S(1)}, f32[4,128,256]{1,2,0:T(8,128)}) fusion(bf16[128,4,64]{0,2,1:T(8,128)(2,1)S(1)} %bitcast.191, bf16[256,4,64]{0,2,1:T(8,128)(2,1)S(1)} %bitcast.178, pred[128,256]{0,1:T(8,128)(4,1)S(1)} %copy-done.16), kind=kOutput, calls=%fused_computation.172 | convolution fusion | flops 17432832 | bytes 755712 | tf_op jit(solution)/shard_map/sub | solution.py:64
  51.4 1.3 %fusion.68 = f32[4,256,64]{1,2,0:T(8,128)} fusion(bf16[128,4,64]{0,2,1:T(8,128)(2,1)S(1)} %bitcast.168, f32[4,128]{1,0:T(4,128)S(1)} %get-tuple-element.119, pred[128,256]{0,1:T(8,128)(4,1)S(1)} %copy-done.15, bf16[128,4,64]{0,2,1:T(8,128)(2,1)S(1)} %bitcast.189, bf16[256,4,64]{0,2,1:T(8,128)(2,1)S(1)} %bitcast.176), kind=kOutput, calls=%fused_computation.82 | convolution fusion | flops 34341632 | bytes 559104 | tf_op jit(solution)/shard_map/hqk,qhd->khd/dot_general | solution.py:67
  52.7 1.5 %fusion.44 = f32[4,256,64]{1,2,0:T(8,128)S(1)} fusion(bf16[128,4,64]{0,2,1:T(8,128)(2,1)S(1)} %bitcast.193, f32[4,128,256]{1,2,0:T(8,128)S(1)} %fusion.125, f32[4,128,256]{1,2,0:T(8,128)} %get-tuple-element.118, f32[4,128]{1,0:T(4,128)S(1)} %get-tuple-element.117), kind=kOutput, calls=%fused_computation.56 | convolution fusion | flops 17695488 | bytes 1378304 | tf_op jit(solution)/shard_map/hqk,qhd->khd/dot_general | solution.py:78
  54.3 1.0 fusion.43
  55.4 0.9 copy-done.3
  57.6 1.3 %collective-permute-start.2 = (f32[64,512]{0,1:T(8,128)S(1)}, f32[64,512]{0,1:T(8,128)S(1)}, u32[]{:S(2)}, u32[]{:S(2)}) collective-permute-start(f32[64,512]{0,1:T(8,128)S(1)} %slice.255), channel_id=1, source_target_pairs={{0,4},{4,8},{8,12},{12,16},{16,20},{20,24},{24,28},{1,5},{5,9},{9,... | collective-permute-start | bytes 393224 | tf_op jit(solution)/shard_map/ppermute | solution.py:26
  59.0 1.5 %convolution_convert_fusion = bf16[4,128,64]{1,2,0:T(8,128)(2,1)S(1)} fusion(bf16[256,4,64]{0,2,1:T(8,128)(2,1)S(1)} %bitcast.180, f32[4,128,256]{1,2,0:T(8,128)S(1)} %fusion.125, f32[4,128,256]{1,2,0:T(8,128)} %get-tuple-element.118, f32[4,128]{1,0:T(4,128)S(1)} %get-tuple-element.117), kind=kOutput, calls=%fused_computation.50 | convolution fusion | flops 17728256 | bytes 1247232 | tf_op jit(solution)/shard_map/hqk,khd->qhd/dot_general | solution.py:75
  60.5 6.9 %collective-permute-done.2 = f32[64,512]{0,1:T(8,128)S(1)} collective-permute-done((f32[64,512]{0,1:T(8,128)S(1)}, f32[64,512]{0,1:T(8,128)S(1)}, u32[]{:S(2)}, u32[]{:S(2)}) %collective-permute-start.2) | collective-permute-done | bytes 131104 | tf_op jit(solution)/shard_map/ppermute | solution.py:26
  67.5 4.2 %collective-permute-start.3 = (f32[64,512]{0,1:T(8,128)S(1)}, f32[64,512]{0,1:T(8,128)S(1)}, u32[]{:S(2)}, u32[]{:S(2)}) collective-permute-start(f32[64,512]{0,1:T(8,128)S(1)} %get-tuple-element.91), channel_id=1, source_target_pairs={{4,0},{8,4},{12,8},{16,12},{20,16},{24,20},{28,24},{5,1},{9,5},{13... | collective-permute-start | bytes 393224 | tf_op jit(solution)/shard_map/ppermute | solution.py:26
  71.8 1.5 %convolution_convert_fusion.1 = bf16[4,128,64]{1,2,0:T(8,128)(2,1)S(1)} fusion(bf16[256,4,64]{0,2,1:T(8,128)(2,1)S(1)} %bitcast.177, f32[4,128,256]{1,2,0:T(8,128)S(1)} %fusion.124, f32[4,128,256]{1,2,0:T(8,128)} %copy-done.18, f32[4,128]{1,0:T(4,128)S(1)} %get-tuple-element.119), kind=kOutput, calls=%fused_computation.51 | convolution fusion | flops 17728256 | bytes 1247232 | tf_op jit(solution)/shard_map/hqk,khd->qhd/dot_general | solution.py:75
  75.0 3.4 %all-to-all-start.4 = ((bf16[4,128,256]{2,1,0:T(8,128)(2,1)}), bf16[4,128,256]{2,1,0:T(8,128)(2,1)S(1)}, u32[]{:S(2)}, u32[]{:S(2)}) async-start(bf16[4,128,256]{2,1,0:T(8,128)(2,1)} %bitcast.42), calls=%async_computation.4 | async-start | bytes 524288 | tf_op jit(solution)/shard_map/all_to_all | solution.py:113
  78.5 1.9 %scatter-add.26 = f32[512,512]{0,1:T(8,128)S(1)} dynamic-update-slice(f32[512,512]{0,1:T(8,128)S(1)} %slice.253, f32[64,512]{0,1:T(8,128)S(1)} %get-tuple-element.92, s32[]{:T(128)} %constant.187.clone.1, s32[]{:T(128)} %constant.187.clone.1) | dynamic-update-slice | bytes 262148 | tf_op jit(solution)/shard_map/scatter-add | solution.py:111
  80.5 1.5 %scatter-add.29 = f32[512,512]{0,1:T(8,128)S(1)} dynamic-update-slice(f32[512,512]{0,1:T(8,128)S(1)} %scatter-add.26, f32[64,512]{0,1:T(8,128)S(1)} %slice_add_fusion.3, s32[]{:T(128)} %constant.198.clone.1, s32[]{:T(128)} %constant.187.clone.1) | dynamic-update-slice | bytes 262148 | tf_op jit(solution)/shard_map/scatter-add | solution.py:111
  83.0 1.5 %all-to-all-done.4 = bf16[4,128,256]{2,1,0:T(8,128)(2,1)S(1)} async-done(((bf16[4,128,256]{2,1,0:T(8,128)(2,1)}), bf16[4,128,256]{2,1,0:T(8,128)(2,1)S(1)}, u32[]{:S(2)}, u32[]{:S(2)}) %all-to-all-start.4) | async-done | bytes 262176 | tf_op jit(solution)/shard_map/all_to_all | solution.py:113
  84.5 3.4 %all-to-all-start.6 = ((bf16[4,128,256]{2,1,0:T(8,128)(2,1)}), bf16[4,128,256]{2,1,0:T(8,128)(2,1)S(1)}, u32[]{:S(2)}, u32[]{:S(2)}) async-start(bf16[4,128,256]{2,1,0:T(8,128)(2,1)} %bitcast.64), calls=%async_computation.6 | async-start | bytes 524288 | tf_op jit(solution)/shard_map/all_to_all | solution.py:123
  88.7 5.2 %all-to-all-done.6 = bf16[4,128,256]{2,1,0:T(8,128)(2,1)S(1)} async-done(((bf16[4,128,256]{2,1,0:T(8,128)(2,1)}), bf16[4,128,256]{2,1,0:T(8,128)(2,1)S(1)}, u32[]{:S(2)}, u32[]{:S(2)}) %all-to-all-start.6) | async-done | bytes 262176 | tf_op jit(solution)/shard_map/all_to_all | solution.py:123
  93.9 3.4 %all-to-all-start.5 = ((bf16[4,128,256]{2,1,0:T(8,128)(2,1)}), bf16[4,128,256]{2,1,0:T(8,128)(2,1)S(1)}, u32[]{:S(2)}, u32[]{:S(2)}) async-start(bf16[4,128,256]{2,1,0:T(8,128)(2,1)} %bitcast.61), calls=%async_computation.5 | async-start | bytes 524288 | tf_op jit(solution)/shard_map/all_to_all | solution.py:116
  99.4 3.9 %all-to-all-done.5 = bf16[4,128,256]{2,1,0:T(8,128)(2,1)S(1)} async-done(((bf16[4,128,256]{2,1,0:T(8,128)(2,1)}), bf16[4,128,256]{2,1,0:T(8,128)(2,1)S(1)}, u32[]{:S(2)}, u32[]{:S(2)}) %all-to-all-start.5) | async-done | bytes 262176 | tf_op jit(solution)/shard_map/all_to_all | solution.py:116
  (95 shorter events, 19.0 us)
Async XLA Ops:
  0.6 5.6 %copy-start = (bf16[128,1024]{1,0:T(8,128)(2,1)S(1)}, bf16[128,1024]{1,0:T(8,128)(2,1)}, u32[]{:S(2)}) copy-start(bf16[128,1024]{1,0:T(8,128)(2,1)} %param.17) | copy-start | bytes 786436
  0.6 6.4 %copy-start.1 = (bf16[128,1024]{1,0:T(8,128)(2,1)S(1)}, bf16[128,1024]{1,0:T(8,128)(2,1)}, u32[]{:S(2)}) copy-start(bf16[128,1024]{1,0:T(8,128)(2,1)} %param.19) | copy-start | bytes 786436
  1.8 6.3 %copy-start.17 = (s32[4]{0:T(128)S(1)}, s32[4]{0:T(128)}, u32[]{:S(2)}) copy-start(s32[4]{0:T(128)} %param.21) | copy-start | bytes 52
  2.7 9.4 %all-to-all-start = ((bf16[128,4,256]{2,0,1:T(8,128)(2,1)}), bf16[128,4,256]{2,0,1:T(8,128)(2,1)S(1)}, u32[]{:S(2)}, u32[]{:S(2)}) async-start(bf16[128,4,256]{2,0,1:T(8,128)(2,1)} %copy.102), calls=%async_computation | async-start | bytes 524288 | tf_op jit(solution)/shard_map/all_to_all | solution.py:96
  6.2 18.9 %copy-start.2 = (bf16[128,1024]{1,0:T(8,128)(2,1)S(1)}, bf16[128,1024]{1,0:T(8,128)(2,1)}, u32[]{:S(2)}) copy-start(bf16[128,1024]{1,0:T(8,128)(2,1)} %param.20) | copy-start | bytes 786436
  12.1 9.4 %all-to-all-start.1 = ((bf16[128,4,256]{2,0,1:T(8,128)(2,1)}), bf16[128,4,256]{2,0,1:T(8,128)(2,1)S(1)}, u32[]{:S(2)}, u32[]{:S(2)}) async-start(bf16[128,4,256]{2,0,1:T(8,128)(2,1)} %copy.104), calls=%async_computation.1 | async-start | bytes 524288 | tf_op jit(solution)/shard_map/all_to_all | solution.py:97
  21.5 10.7 %all-to-all-start.2 = ((bf16[128,4,256]{0,2,1:T(8,128)(2,1)}), bf16[128,4,256]{0,2,1:T(8,128)(2,1)S(1)}, u32[]{:S(2)}, u32[]{:S(2)}) async-start(bf16[128,4,256]{0,2,1:T(8,128)(2,1)} %bitcast.9), calls=%async_computation.2 | async-start | bytes 524288 | tf_op jit(solution)/shard_map/all_to_all | solution.py:95
  26.4 15.3 %collective-permute-start = (bf16[64,512]{0,1:T(8,128)(2,1)S(1)}, bf16[64,512]{0,1:T(8,128)(2,1)S(1)}, u32[]{:S(2)}, u32[]{:S(2)}) collective-permute-start(bf16[64,512]{0,1:T(8,128)(2,1)S(1)} %get-tuple-element.101), channel_id=1, source_target_pairs={{0,4},{4,8},{8,12},{12,16},{16,20},{20,24},{24,28},{1,5},{5,9},{9,... | collective-permute-start | bytes 196616 | tf_op jit(solution)/shard_map/ppermute | solution.py:15
  27.7 14.0 %collective-permute-start.1 = (bf16[64,512]{0,1:T(8,128)(2,1)S(1)}, bf16[64,512]{0,1:T(8,128)(2,1)S(1)}, u32[]{:S(2)}, u32[]{:S(2)}) collective-permute-start(bf16[64,512]{0,1:T(8,128)(2,1)S(1)} %get-tuple-element.102), channel_id=1, source_target_pairs={{4,0},{8,4},{12,8},{16,12},{20,16},{24,20},{28,24},{5,1},{9,5},{13... | collective-permute-start | bytes 196616 | tf_op jit(solution)/shard_map/ppermute | solution.py:18
  32.2 9.4 %all-to-all-start.3 = ((bf16[128,4,256]{0,2,1:T(8,128)(2,1)}), bf16[128,4,256]{0,2,1:T(8,128)(2,1)S(1)}, u32[]{:S(2)}, u32[]{:S(2)}) async-start(bf16[128,4,256]{0,2,1:T(8,128)(2,1)} %bitcast.14), calls=%async_computation.3 | async-start | bytes 524288 | tf_op jit(solution)/shard_map/all_to_all | solution.py:98
  35.7 14.4 %copy-start.12 = (bf16[1,128,256]{1,2,0:T(8,128)(2,1)}, bf16[1,128,256]{1,2,0:T(8,128)(2,1)S(1)}, u32[]{:S(2)}) copy-start(bf16[1,128,256]{1,2,0:T(8,128)(2,1)S(1)} %get-tuple-element.105) | copy-start | bytes 196612
  35.7 15.7 %copy-start.10 = (bf16[1,128,256]{1,2,0:T(8,128)(2,1)}, bf16[1,128,256]{1,2,0:T(8,128)(2,1)S(1)}, u32[]{:S(2)}) copy-start(bf16[1,128,256]{1,2,0:T(8,128)(2,1)S(1)} %get-tuple-element.106) | copy-start | bytes 196612
  42.3 7.9 %copy-start.7 = (bf16[256,256]{0,1:T(8,128)(2,1)}, bf16[256,256]{0,1:T(8,128)(2,1)S(1)}, u32[]{:S(2)}) copy-start(bf16[256,256]{0,1:T(8,128)(2,1)S(1)} %get-tuple-element.111) | copy-start | bytes 393220
  47.4 1.6 %copy-start.16 = (pred[128,256]{0,1:T(8,128)(4,1)S(1)}, pred[128,256]{0,1:T(8,128)(4,1)}, u32[]{:S(2)}) copy-start(pred[128,256]{0,1:T(8,128)(4,1)} %fusion.85) | copy-start | bytes 98308
  50.1 0.9 copy-start.15
  51.4 2.8 %copy-start.18 = (f32[4,128,256]{1,2,0:T(8,128)}, f32[4,128,256]{1,2,0:T(8,128)S(1)}, u32[]{:S(2)}) copy-start(f32[4,128,256]{1,2,0:T(8,128)S(1)} %get-tuple-element.120) | copy-start | bytes 1572868
  51.4 1.3 %copy-start.13 = (bf16[1,128,256]{1,2,0:T(8,128)(2,1)S(1)}, bf16[1,128,256]{1,2,0:T(8,128)(2,1)}, u32[]{:S(2)}) copy-start(bf16[1,128,256]{1,2,0:T(8,128)(2,1)} %copy-done.12) | copy-start | bytes 196612
  52.7 1.6 %copy-start.11 = (bf16[1,128,256]{1,2,0:T(8,128)(2,1)S(1)}, bf16[1,128,256]{1,2,0:T(8,128)(2,1)}, u32[]{:S(2)}) copy-start(bf16[1,128,256]{1,2,0:T(8,128)(2,1)} %copy-done.10) | copy-start | bytes 196612
  55.3 0.9 copy-start.3
  55.3 1.0 copy-start.4
  56.3 0.9 copy-start.5
  56.3 1.0 copy-start.6
  57.3 1.6 %copy-start.8 = (bf16[256,256]{0,1:T(8,128)(2,1)S(1)}, bf16[256,256]{0,1:T(8,128)(2,1)}, u32[]{:S(2)}) copy-start(bf16[256,256]{0,1:T(8,128)(2,1)} %copy-done.7) | copy-start | bytes 393220
  57.6 9.7 %collective-permute-start.2 = (f32[64,512]{0,1:T(8,128)S(1)}, f32[64,512]{0,1:T(8,128)S(1)}, u32[]{:S(2)}, u32[]{:S(2)}) collective-permute-start(f32[64,512]{0,1:T(8,128)S(1)} %slice.255), channel_id=1, source_target_pairs={{0,4},{4,8},{8,12},{12,16},{16,20},{20,24},{24,28},{1,5},{5,9},{9,... | collective-permute-start | bytes 393224 | tf_op jit(solution)/shard_map/ppermute | solution.py:26
  67.5 12.9 %collective-permute-start.3 = (f32[64,512]{0,1:T(8,128)S(1)}, f32[64,512]{0,1:T(8,128)S(1)}, u32[]{:S(2)}, u32[]{:S(2)}) collective-permute-start(f32[64,512]{0,1:T(8,128)S(1)} %get-tuple-element.91), channel_id=1, source_target_pairs={{4,0},{8,4},{12,8},{16,12},{20,16},{24,20},{28,24},{5,1},{9,5},{13... | collective-permute-start | bytes 393224 | tf_op jit(solution)/shard_map/ppermute | solution.py:26
  73.3 0.8 copy-start.9
  73.3 0.9 copy-start.14
  75.0 9.4 %all-to-all-start.4 = ((bf16[4,128,256]{2,1,0:T(8,128)(2,1)}), bf16[4,128,256]{2,1,0:T(8,128)(2,1)S(1)}, u32[]{:S(2)}, u32[]{:S(2)}) async-start(bf16[4,128,256]{2,1,0:T(8,128)(2,1)} %bitcast.42), calls=%async_computation.4 | async-start | bytes 524288 | tf_op jit(solution)/shard_map/all_to_all | solution.py:113
  84.5 9.4 %all-to-all-start.6 = ((bf16[4,128,256]{2,1,0:T(8,128)(2,1)}), bf16[4,128,256]{2,1,0:T(8,128)(2,1)S(1)}, u32[]{:S(2)}, u32[]{:S(2)}) async-start(bf16[4,128,256]{2,1,0:T(8,128)(2,1)} %bitcast.64), calls=%async_computation.6 | async-start | bytes 524288 | tf_op jit(solution)/shard_map/all_to_all | solution.py:123
  93.9 9.4 %all-to-all-start.5 = ((bf16[4,128,256]{2,1,0:T(8,128)(2,1)}), bf16[4,128,256]{2,1,0:T(8,128)(2,1)S(1)}, u32[]{:S(2)}, u32[]{:S(2)}) async-start(bf16[4,128,256]{2,1,0:T(8,128)(2,1)} %bitcast.61), calls=%async_computation.5 | async-start | bytes 524288 | tf_op jit(solution)/shard_map/all_to_all | solution.py:116
where the time goes:
time: 105 us; the launch traced here: 104 us
  starting transfers between devices  35.2 us (34%)
  waiting for transfers between devices  31.4 us (30%)
  local copies, waits for them, and re-layouts  16.8 us (16%)
  matrix products  15.9 us (15%)
  other arithmetic  3.8 us (4%)
  between operations  1.16 us (1%)
    ppermute x2, waiting for transfers between devices, shifted(): return lax.ppermute(block, axis, route)  6.94 us
    unnamed x43, local copies, waits for them, and re-layouts  6.22 us
    all_to_all x1, waiting for transfers between devices, body(): lax.all_to_all(grad_output, 'head', split_axis=1, concat_axis=0, tiled=True)  5.95 us
    ppermute x2, starting transfers between devices, shifted(): return lax.ppermute(block, axis, route)  5.54 us
    all_to_all x1, waiting for transfers between devices, body(): lax.all_to_all(value_vectors, 'head', split_axis=1, concat_axis=0, tiled=...  5.22 us
    all_to_all x1, waiting for transfers between devices, body(): lax.all_to_all(own_rows[:, columns:].astype(jnp.bfloat16), 'head', split_...  5.16 us
    dot_general x4, matrix products, band_grads(): jnp.einsum('hqk,khd->qhd', score_grad, key_block, preferred_element_type=...  4.84 us
    ppermute x1, starting transfers between devices, with_halo(): lax.ppermute(lax.slice_in_dim(block, 0, width, axis=dim), axis, backward)  4.55 us
  transfers between devices with their start and end apart: 11, of which 7 were waited for; matrix products, arithmetic and copies ran while one was open for 16% of the time, Pallas kernels for 0%

commit v1 on v0

--- a/solution.py
+++ b/solution.py
@@ -1,3 +1,4 @@
+import functools
 import jax
 import jax.numpy as jnp
 from jax import lax
@@ -5,6 +6,21 @@
 
 DH = 64
 WIN = 64
+
+
+def run_yards(piece_in, dev_axis):
+    return jnp.concatenate(
+        lax.all_to_all(
+            jnp.stack(jnp.split(piece_in, lax.axis_size(dev_axis), 0), 0),
+            axis_name=dev_axis,
+            split_axis=0,
+            concat_axis=0,
+        ),
+        1,
+    )
+
+
+map_skins = functools.partial(run_yards, dev_axis="head")
 
 
 def with_halo(block, sides, width):
@@ -120,13 +136,7 @@
             concat_axis=1,
             tiled=True,
         ),
-        lax.all_to_all(
-            own_rows[:, columns:].astype(jnp.bfloat16),
-            "head",
-            split_axis=0,
-            concat_axis=1,
-            tiled=True,
-        ),
+        map_skins(own_rows[:, columns:].astype(jnp.bfloat16)),
     )
     return (outputs[0], outputs[1], outputs[2])
 

time: 105 us -> 105 us (level)
    all_to_all x1, waiting for transfers between devices: 3.94 us -> 5.21 us  [body(): lax.all_to_all(own_rows[:, :columns].astype(jnp.bfloat16), 'head', split_...]
    all_to_all x1, waiting for transfers between devices: 5.16 us -> 3.94 us  [run_yards(): lax.all_to_all(jnp.stack(jnp.split(piece_in, lax.axis_size(dev_axis), 0),...]
    unnamed x43 -> x42, local copies, waits for them, and re-layouts: 6.22 us -> 5.37 us
where the time goes in v1:
time: 105 us; the launch traced here: 104 us
  starting transfers between devices  35.2 us (34%)
  waiting for transfers between devices  31.5 us (30%)
  matrix products  15.9 us (15%)
  local copies, waits for them, and re-layouts  15.8 us (15%)
  other arithmetic  4.53 us (4%)
  between operations  1.16 us (1%)
    ppermute x2, waiting for transfers between devices, shifted(): return lax.ppermute(block, axis, route)  6.94 us
    all_to_all x1, waiting for transfers between devices, body(): lax.all_to_all(grad_output, 'head', split_axis=1, concat_axis=0, tiled=True)  5.95 us
    ppermute x2, starting transfers between devices, shifted(): return lax.ppermute(block, axis, route)  5.54 us
    unnamed x42, local copies, waits for them, and re-layouts  5.37 us
    all_to_all x1, waiting for transfers between devices, body(): lax.all_to_all(value_vectors, 'head', split_axis=1, concat_axis=0, tiled=...  5.22 us
    all_to_all x1, waiting for transfers between devices, body(): lax.all_to_all(own_rows[:, :columns].astype(jnp.bfloat16), 'head', split_...  5.21 us
    dot_general x4, matrix products, band_grads(): jnp.einsum('hqk,khd->qhd', score_grad, key_block, preferred_element_type=...  4.84 us
    ppermute x1, starting transfers between devices, with_halo(): lax.ppermute(lax.slice_in_dim(block, 0, width, axis=dim), axis, backward)  4.55 us
  transfers between devices with their start and end apart: 11, of which 7 were waited for; matrix products, arithmetic and copies ran while one was open for 16% of the time, Pallas kernels for 0%

profile of v1, /device:TPU:26, one launch (start us, length us, event | category | flops | bytes accessed | tf_op | source)
XLA Modules:
  0.0 104.2 jit_solution(11933426857336777404)
XLA Ops:
  0.7 1.2 %copy.99 = bf16[128,1024]{0,1:T(8,128)(2,1)S(1)} copy(bf16[128,1024]{1,0:T(8,128)(2,1)} %param.18) | data formatting | bytes 524288 | tf_op args[1]
  2.7 3.4 %all-to-all-start = ((bf16[128,4,256]{2,0,1:T(8,128)(2,1)}), bf16[128,4,256]{2,0,1:T(8,128)(2,1)S(1)}, u32[]{:S(2)}, u32[]{:S(2)}) async-start(bf16[128,4,256]{2,0,1:T(8,128)(2,1)} %copy.100), calls=%async_computation | async-start | bytes 524288 | tf_op jit(solution)/shard_map/all_to_all | solution.py:112
  9.4 2.7 %all-to-all-done = bf16[128,4,256]{2,0,1:T(8,128)(2,1)S(1)} async-done(((bf16[128,4,256]{2,0,1:T(8,128)(2,1)}), bf16[128,4,256]{2,0,1:T(8,128)(2,1)S(1)}, u32[]{:S(2)}, u32[]{:S(2)}) %all-to-all-start) | async-done | bytes 262176 | tf_op jit(solution)/shard_map/all_to_all | solution.py:112
  12.1 3.4 %all-to-all-start.1 = ((bf16[128,4,256]{2,0,1:T(8,128)(2,1)}), bf16[128,4,256]{2,0,1:T(8,128)(2,1)S(1)}, u32[]{:S(2)}, u32[]{:S(2)}) async-start(bf16[128,4,256]{2,0,1:T(8,128)(2,1)} %copy.102), calls=%async_computation.1 | async-start | bytes 524288 | tf_op jit(solution)/shard_map/all_to_all | solution.py:113
  16.3 5.2 %all-to-all-done.1 = bf16[128,4,256]{2,0,1:T(8,128)(2,1)S(1)} async-done(((bf16[128,4,256]{2,0,1:T(8,128)(2,1)}), bf16[128,4,256]{2,0,1:T(8,128)(2,1)S(1)}, u32[]{:S(2)}, u32[]{:S(2)}) %all-to-all-start.1) | async-done | bytes 262176 | tf_op jit(solution)/shard_map/all_to_all | solution.py:113
  21.5 3.4 %all-to-all-start.2 = ((bf16[128,4,256]{0,2,1:T(8,128)(2,1)}), bf16[128,4,256]{0,2,1:T(8,128)(2,1)S(1)}, u32[]{:S(2)}, u32[]{:S(2)}) async-start(bf16[128,4,256]{0,2,1:T(8,128)(2,1)} %bitcast.9), calls=%async_computation.2 | async-start | bytes 524288 | tf_op jit(solution)/shard_map/all_to_all | solution.py:111
  26.4 1.3 %collective-permute-start = (bf16[64,512]{0,1:T(8,128)(2,1)S(1)}, bf16[64,512]{0,1:T(8,128)(2,1)S(1)}, u32[]{:S(2)}, u32[]{:S(2)}) collective-permute-start(bf16[64,512]{0,1:T(8,128)(2,1)S(1)} %get-tuple-element.103), channel_id=1, source_target_pairs={{0,4},{4,8},{8,12},{12,16},{16,20},{20,24},{24,28},{1,5},{5,9},{9,... | collective-permute-start | bytes 196616 | tf_op jit(solution)/shard_map/ppermute | solution.py:31
  27.7 4.6 %collective-permute-start.1 = (bf16[64,512]{0,1:T(8,128)(2,1)S(1)}, bf16[64,512]{0,1:T(8,128)(2,1)S(1)}, u32[]{:S(2)}, u32[]{:S(2)}) collective-permute-start(bf16[64,512]{0,1:T(8,128)(2,1)S(1)} %get-tuple-element.104), channel_id=1, source_target_pairs={{4,0},{8,4},{12,8},{16,12},{20,16},{24,20},{28,24},{5,1},{9,5},{13... | collective-permute-start | bytes 196616 | tf_op jit(solution)/shard_map/ppermute | solution.py:34
  32.2 3.4 %all-to-all-start.3 = ((bf16[128,4,256]{0,2,1:T(8,128)(2,1)}), bf16[128,4,256]{0,2,1:T(8,128)(2,1)S(1)}, u32[]{:S(2)}, u32[]{:S(2)}) async-start(bf16[128,4,256]{0,2,1:T(8,128)(2,1)} %bitcast.14), calls=%async_computation.3 | async-start | bytes 524288 | tf_op jit(solution)/shard_map/all_to_all | solution.py:114
  35.7 6.0 %all-to-all-done.3 = bf16[128,4,256]{0,2,1:T(8,128)(2,1)S(1)} async-done(((bf16[128,4,256]{0,2,1:T(8,128)(2,1)}), bf16[128,4,256]{0,2,1:T(8,128)(2,1)S(1)}, u32[]{:S(2)}, u32[]{:S(2)}) %all-to-all-start.3) | async-done | bytes 262176 | tf_op jit(solution)/shard_map/all_to_all | solution.py:114
  43.0 0.9 convolution_convert_fusion.3
  45.4 0.9 convolution_convert_fusion.2
  46.4 1.0 fusion.45
  47.4 1.3 %fusion.64 = f32[4,256,64]{1,2,0:T(8,128)} fusion(bf16[128,4,64]{0,2,1:T(8,128)(2,1)S(1)} %bitcast.179, f32[4,128]{1,0:T(4,128)S(1)} %get-tuple-element.117, pred[128,256]{0,1:T(8,128)(4,1)S(1)} %fusion.84, bf16[256,4,64]{0,2,1:T(8,128)(2,1)S(1)} %bitcast.190, bf16[128,4,64]{0,2,1:T(8,128)(2,1)S(1)} %bitcast.204), kind=kOutput, calls=%fused_computation.79 | convolution fusion | flops 34341632 | bytes 559104 | tf_op jit(solution)/shard_map/hqk,qhd->khd/dot_general | solution.py:83
  48.9 1.2 %fusion.120 = (f32[4,128]{1,0:T(4,128)S(1)}, f32[4,128,256]{1,2,0:T(8,128)}) fusion(bf16[128,4,64]{0,2,1:T(8,128)(2,1)S(1)} %bitcast.198, bf16[256,4,64]{0,2,1:T(8,128)(2,1)S(1)} %bitcast.185, pred[128,256]{0,1:T(8,128)(4,1)S(1)} %copy-done.16), kind=kOutput, calls=%fused_computation.176 | convolution fusion | flops 17432832 | bytes 755712 | tf_op jit(solution)/shard_map/sub | solution.py:80
  51.4 1.3 %fusion.68 = f32[4,256,64]{1,2,0:T(8,128)} fusion(bf16[128,4,64]{0,2,1:T(8,128)(2,1)S(1)} %bitcast.175, f32[4,128]{1,0:T(4,128)S(1)} %get-tuple-element.121, pred[128,256]{0,1:T(8,128)(4,1)S(1)} %copy-done.15, bf16[128,4,64]{0,2,1:T(8,128)(2,1)S(1)} %bitcast.196, bf16[256,4,64]{0,2,1:T(8,128)(2,1)S(1)} %bitcast.183), kind=kOutput, calls=%fused_computation.83 | convolution fusion | flops 34341632 | bytes 559104 | tf_op jit(solution)/shard_map/hqk,qhd->khd/dot_general | solution.py:83
  52.7 1.5 %fusion.44 = f32[4,256,64]{1,2,0:T(8,128)S(1)} fusion(bf16[128,4,64]{0,2,1:T(8,128)(2,1)S(1)} %bitcast.200, f32[4,128,256]{1,2,0:T(8,128)S(1)} %fusion.124, f32[4,128,256]{1,2,0:T(8,128)} %get-tuple-element.120, f32[4,128]{1,0:T(4,128)S(1)} %get-tuple-element.119), kind=kOutput, calls=%fused_computation.56 | convolution fusion | flops 17695488 | bytes 1378304 | tf_op jit(solution)/shard_map/hqk,qhd->khd/dot_general | solution.py:94
  54.3 1.0 fusion.43
  55.4 0.9 copy-done.3
  57.6 1.3 %collective-permute-start.2 = (f32[64,512]{0,1:T(8,128)S(1)}, f32[64,512]{0,1:T(8,128)S(1)}, u32[]{:S(2)}, u32[]{:S(2)}) collective-permute-start(f32[64,512]{0,1:T(8,128)S(1)} %slice.256), channel_id=1, source_target_pairs={{0,4},{4,8},{8,12},{12,16},{16,20},{20,24},{24,28},{1,5},{5,9},{9,... | collective-permute-start | bytes 393224 | tf_op jit(solution)/shard_map/ppermute | solution.py:42
  59.0 1.5 %convolution_convert_fusion = bf16[4,128,64]{1,2,0:T(8,128)(2,1)S(1)} fusion(bf16[256,4,64]{0,2,1:T(8,128)(2,1)S(1)} %bitcast.187, f32[4,128,256]{1,2,0:T(8,128)S(1)} %fusion.124, f32[4,128,256]{1,2,0:T(8,128)} %get-tuple-element.120, f32[4,128]{1,0:T(4,128)S(1)} %get-tuple-element.119), kind=kOutput, calls=%fused_computation.50 | convolution fusion | flops 17728256 | bytes 1247232 | tf_op jit(solution)/shard_map/hqk,khd->qhd/dot_general | solution.py:91
  60.5 6.9 %collective-permute-done.2 = f32[64,512]{0,1:T(8,128)S(1)} collective-permute-done((f32[64,512]{0,1:T(8,128)S(1)}, f32[64,512]{0,1:T(8,128)S(1)}, u32[]{:S(2)}, u32[]{:S(2)}) %collective-permute-start.2) | collective-permute-done | bytes 131104 | tf_op jit(solution)/shard_map/ppermute | solution.py:42
  67.5 4.2 %collective-permute-start.3 = (f32[64,512]{0,1:T(8,128)S(1)}, f32[64,512]{0,1:T(8,128)S(1)}, u32[]{:S(2)}, u32[]{:S(2)}) collective-permute-start(f32[64,512]{0,1:T(8,128)S(1)} %get-tuple-element.91), channel_id=1, source_target_pairs={{4,0},{8,4},{12,8},{16,12},{20,16},{24,20},{28,24},{5,1},{9,5},{13... | collective-permute-start | bytes 393224 | tf_op jit(solution)/shard_map/ppermute | solution.py:42
  71.8 1.5 %convolution_convert_fusion.1 = bf16[4,128,64]{1,2,0:T(8,128)(2,1)S(1)} fusion(bf16[256,4,64]{0,2,1:T(8,128)(2,1)S(1)} %bitcast.184, f32[4,128,256]{1,2,0:T(8,128)S(1)} %fusion.123, f32[4,128,256]{1,2,0:T(8,128)} %copy-done.18, f32[4,128]{1,0:T(4,128)S(1)} %get-tuple-element.121), kind=kOutput, calls=%fused_computation.51 | convolution fusion | flops 17728256 | bytes 1247232 | tf_op jit(solution)/shard_map/hqk,khd->qhd/dot_general | solution.py:91
  75.0 3.4 %all-to-all-start.4 = ((bf16[4,128,256]{2,1,0:T(8,128)(2,1)}), bf16[4,128,256]{2,1,0:T(8,128)(2,1)S(1)}, u32[]{:S(2)}, u32[]{:S(2)}) async-start(bf16[4,128,256]{2,1,0:T(8,128)(2,1)} %bitcast.42), calls=%async_computation.4 | async-start | bytes 524288 | tf_op jit(solution)/shard_map/all_to_all | solution.py:129
  78.5 1.9 %scatter-add.26 = f32[512,512]{0,1:T(8,128)S(1)} dynamic-update-slice(f32[512,512]{0,1:T(8,128)S(1)} %slice.254, f32[64,512]{0,1:T(8,128)S(1)} %get-tuple-element.92, s32[]{:T(128)} %constant.187.clone.1, s32[]{:T(128)} %constant.187.clone.1) | dynamic-update-slice | bytes 262148 | tf_op jit(solution)/shard_map/scatter-add | solution.py:127
  80.5 1.5 %scatter-add.29 = f32[512,512]{0,1:T(8,128)S(1)} dynamic-update-slice(f32[512,512]{0,1:T(8,128)S(1)} %scatter-add.26, f32[64,512]{0,1:T(8,128)S(1)} %slice_add_fusion.3, s32[]{:T(128)} %constant.198.clone.1, s32[]{:T(128)} %constant.187.clone.1) | dynamic-update-slice | bytes 262148 | tf_op jit(solution)/shard_map/scatter-add | solution.py:127
  83.0 1.5 %all-to-all-done.4 = bf16[4,128,256]{2,1,0:T(8,128)(2,1)S(1)} async-done(((bf16[4,128,256]{2,1,0:T(8,128)(2,1)}), bf16[4,128,256]{2,1,0:T(8,128)(2,1)S(1)}, u32[]{:S(2)}, u32[]{:S(2)}) %all-to-all-start.4) | async-done | bytes 262176 | tf_op jit(solution)/shard_map/all_to_all | solution.py:129
  84.5 3.4 %all-to-all-start.5 = ((bf16[4,128,256]{2,1,0:T(8,128)(2,1)}), bf16[4,128,256]{2,1,0:T(8,128)(2,1)S(1)}, u32[]{:S(2)}, u32[]{:S(2)}) async-start(bf16[4,128,256]{2,1,0:T(8,128)(2,1)} %bitcast.61), calls=%async_computation.5 | async-start | bytes 524288 | tf_op jit(solution)/shard_map/all_to_all | solution.py:132
  88.7 5.2 %all-to-all-done.5 = bf16[4,128,256]{2,1,0:T(8,128)(2,1)S(1)} async-done(((bf16[4,128,256]{2,1,0:T(8,128)(2,1)}), bf16[4,128,256]{2,1,0:T(8,128)(2,1)S(1)}, u32[]{:S(2)}, u32[]{:S(2)}) %all-to-all-start.5) | async-done | bytes 262176 | tf_op jit(solution)/shard_map/all_to_all | solution.py:132
  93.9 3.4 %all-to-all-start.6 = ((bf16[4,128,256]{1,2,0:T(8,128)(2,1)}), bf16[4,128,256]{1,2,0:T(8,128)(2,1)S(1)}, u32[]{:S(2)}, u32[]{:S(2)}) async-start(bf16[4,128,256]{1,2,0:T(8,128)(2,1)} %pad_maximum_fusion.1), calls=%async_computation.6 | async-start | bytes 524288 | tf_op jit(solution)/shard_map/all_to_all | solution.py:13
  99.4 3.9 %all-to-all-done.6 = bf16[4,128,256]{1,2,0:T(8,128)(2,1)S(1)} async-done(((bf16[4,128,256]{1,2,0:T(8,128)(2,1)}), bf16[4,128,256]{1,2,0:T(8,128)(2,1)S(1)}, u32[]{:S(2)}, u32[]{:S(2)}) %all-to-all-start.6) | async-done | bytes 262176 | tf_op jit(solution)/shard_map/all_to_all | solution.py:13
  (95 shorter events, 18.7 us)
Async XLA Ops:
  0.6 5.6 %copy-start = (bf16[128,1024]{1,0:T(8,128)(2,1)S(1)}, bf16[128,1024]{1,0:T(8,128)(2,1)}, u32[]{:S(2)}) copy-start(bf16[128,1024]{1,0:T(8,128)(2,1)} %param.17) | copy-start | bytes 786436
  0.6 6.4 %copy-start.1 = (bf16[128,1024]{1,0:T(8,128)(2,1)S(1)}, bf16[128,1024]{1,0:T(8,128)(2,1)}, u32[]{:S(2)}) copy-start(bf16[128,1024]{1,0:T(8,128)(2,1)} %param.19) | copy-start | bytes 786436
  1.8 6.3 %copy-start.17 = (s32[4]{0:T(128)S(1)}, s32[4]{0:T(128)}, u32[]{:S(2)}) copy-start(s32[4]{0:T(128)} %param.21) | copy-start | bytes 52
  2.7 9.4 %all-to-all-start = ((bf16[128,4,256]{2,0,1:T(8,128)(2,1)}), bf16[128,4,256]{2,0,1:T(8,128)(2,1)S(1)}, u32[]{:S(2)}, u32[]{:S(2)}) async-start(bf16[128,4,256]{2,0,1:T(8,128)(2,1)} %copy.100), calls=%async_computation | async-start | bytes 524288 | tf_op jit(solution)/shard_map/all_to_all | solution.py:112
  6.2 18.9 %copy-start.2 = (bf16[128,1024]{1,0:T(8,128)(2,1)S(1)}, bf16[128,1024]{1,0:T(8,128)(2,1)}, u32[]{:S(2)}) copy-start(bf16[128,1024]{1,0:T(8,128)(2,1)} %param.20) | copy-start | bytes 786436
  12.1 9.4 %all-to-all-start.1 = ((bf16[128,4,256]{2,0,1:T(8,128)(2,1)}), bf16[128,4,256]{2,0,1:T(8,128)(2,1)S(1)}, u32[]{:S(2)}, u32[]{:S(2)}) async-start(bf16[128,4,256]{2,0,1:T(8,128)(2,1)} %copy.102), calls=%async_computation.1 | async-start | bytes 524288 | tf_op jit(solution)/shard_map/all_to_all | solution.py:113
  21.5 10.7 %all-to-all-start.2 = ((bf16[128,4,256]{0,2,1:T(8,128)(2,1)}), bf16[128,4,256]{0,2,1:T(8,128)(2,1)S(1)}, u32[]{:S(2)}, u32[]{:S(2)}) async-start(bf16[128,4,256]{0,2,1:T(8,128)(2,1)} %bitcast.9), calls=%async_computation.2 | async-start | bytes 524288 | tf_op jit(solution)/shard_map/all_to_all | solution.py:111
  26.4 15.3 %collective-permute-start = (bf16[64,512]{0,1:T(8,128)(2,1)S(1)}, bf16[64,512]{0,1:T(8,128)(2,1)S(1)}, u32[]{:S(2)}, u32[]{:S(2)}) collective-permute-start(bf16[64,512]{0,1:T(8,128)(2,1)S(1)} %get-tuple-element.103), channel_id=1, source_target_pairs={{0,4},{4,8},{8,12},{12,16},{16,20},{20,24},{24,28},{1,5},{5,9},{9,... | collective-permute-start | bytes 196616 | tf_op jit(solution)/shard_map/ppermute | solution.py:31
  27.7 14.0 %collective-permute-start.1 = (bf16[64,512]{0,1:T(8,128)(2,1)S(1)}, bf16[64,512]{0,1:T(8,128)(2,1)S(1)}, u32[]{:S(2)}, u32[]{:S(2)}) collective-permute-start(bf16[64,512]{0,1:T(8,128)(2,1)S(1)} %get-tuple-element.104), channel_id=1, source_target_pairs={{4,0},{8,4},{12,8},{16,12},{20,16},{24,20},{28,24},{5,1},{9,5},{13... | collective-permute-start | bytes 196616 | tf_op jit(solution)/shard_map/ppermute | solution.py:34
  32.2 9.4 %all-to-all-start.3 = ((bf16[128,4,256]{0,2,1:T(8,128)(2,1)}), bf16[128,4,256]{0,2,1:T(8,128)(2,1)S(1)}, u32[]{:S(2)}, u32[]{:S(2)}) async-start(bf16[128,4,256]{0,2,1:T(8,128)(2,1)} %bitcast.14), calls=%async_computation.3 | async-start | bytes 524288 | tf_op jit(solution)/shard_map/all_to_all | solution.py:114
  35.7 14.4 %copy-start.12 = (bf16[1,128,256]{1,2,0:T(8,128)(2,1)}, bf16[1,128,256]{1,2,0:T(8,128)(2,1)S(1)}, u32[]{:S(2)}) copy-start(bf16[1,128,256]{1,2,0:T(8,128)(2,1)S(1)} %get-tuple-element.107) | copy-start | bytes 196612
  35.7 15.7 %copy-start.10 = (bf16[1,128,256]{1,2,0:T(8,128)(2,1)}, bf16[1,128,256]{1,2,0:T(8,128)(2,1)S(1)}, u32[]{:S(2)}) copy-start(bf16[1,128,256]{1,2,0:T(8,128)(2,1)S(1)} %get-tuple-element.108) | copy-start | bytes 196612
  42.3 7.9 %copy-start.7 = (bf16[256,256]{0,1:T(8,128)(2,1)}, bf16[256,256]{0,1:T(8,128)(2,1)S(1)}, u32[]{:S(2)}) copy-start(bf16[256,256]{0,1:T(8,128)(2,1)S(1)} %get-tuple-element.113) | copy-start | bytes 393220
  47.4 1.6 %copy-start.16 = (pred[128,256]{0,1:T(8,128)(4,1)S(1)}, pred[128,256]{0,1:T(8,128)(4,1)}, u32[]{:S(2)}) copy-start(pred[128,256]{0,1:T(8,128)(4,1)} %fusion.85) | copy-start | bytes 98308
  50.1 0.9 copy-start.15
  51.4 2.8 %copy-start.18 = (f32[4,128,256]{1,2,0:T(8,128)}, f32[4,128,256]{1,2,0:T(8,128)S(1)}, u32[]{:S(2)}) copy-start(f32[4,128,256]{1,2,0:T(8,128)S(1)} %get-tuple-element.122) | copy-start | bytes 1572868
  51.4 1.3 %copy-start.13 = (bf16[1,128,256]{1,2,0:T(8,128)(2,1)S(1)}, bf16[1,128,256]{1,2,0:T(8,128)(2,1)}, u32[]{:S(2)}) copy-start(bf16[1,128,256]{1,2,0:T(8,128)(2,1)} %copy-done.12) | copy-start | bytes 196612
  52.7 1.6 %copy-start.11 = (bf16[1,128,256]{1,2,0:T(8,128)(2,1)S(1)}, bf16[1,128,256]{1,2,0:T(8,128)(2,1)}, u32[]{:S(2)}) copy-start(bf16[1,128,256]{1,2,0:T(8,128)(2,1)} %copy-done.10) | copy-start | bytes 196612
  55.3 0.9 copy-start.3
  55.3 1.0 copy-start.4
  56.3 0.9 copy-start.5
  56.3 1.0 copy-start.6
  57.3 1.6 %copy-start.8 = (bf16[256,256]{0,1:T(8,128)(2,1)S(1)}, bf16[256,256]{0,1:T(8,128)(2,1)}, u32[]{:S(2)}) copy-start(bf16[256,256]{0,1:T(8,128)(2,1)} %copy-done.7) | copy-start | bytes 393220
  57.6 9.7 %collective-permute-start.2 = (f32[64,512]{0,1:T(8,128)S(1)}, f32[64,512]{0,1:T(8,128)S(1)}, u32[]{:S(2)}, u32[]{:S(2)}) collective-permute-start(f32[64,512]{0,1:T(8,128)S(1)} %slice.256), channel_id=1, source_target_pairs={{0,4},{4,8},{8,12},{12,16},{16,20},{20,24},{24,28},{1,5},{5,9},{9,... | collective-permute-start | bytes 393224 | tf_op jit(solution)/shard_map/ppermute | solution.py:42
  67.5 12.9 %collective-permute-start.3 = (f32[64,512]{0,1:T(8,128)S(1)}, f32[64,512]{0,1:T(8,128)S(1)}, u32[]{:S(2)}, u32[]{:S(2)}) collective-permute-start(f32[64,512]{0,1:T(8,128)S(1)} %get-tuple-element.91), channel_id=1, source_target_pairs={{4,0},{8,4},{12,8},{16,12},{20,16},{24,20},{28,24},{5,1},{9,5},{13... | collective-permute-start | bytes 393224 | tf_op jit(solution)/shard_map/ppermute | solution.py:42
  73.3 0.8 copy-start.9
  73.3 0.9 copy-start.14
  75.0 9.4 %all-to-all-start.4 = ((bf16[4,128,256]{2,1,0:T(8,128)(2,1)}), bf16[4,128,256]{2,1,0:T(8,128)(2,1)S(1)}, u32[]{:S(2)}, u32[]{:S(2)}) async-start(bf16[4,128,256]{2,1,0:T(8,128)(2,1)} %bitcast.42), calls=%async_computation.4 | async-start | bytes 524288 | tf_op jit(solution)/shard_map/all_to_all | solution.py:129
  84.5 9.4 %all-to-all-start.5 = ((bf16[4,128,256]{2,1,0:T(8,128)(2,1)}), bf16[4,128,256]{2,1,0:T(8,128)(2,1)S(1)}, u32[]{:S(2)}, u32[]{:S(2)}) async-start(bf16[4,128,256]{2,1,0:T(8,128)(2,1)} %bitcast.61), calls=%async_computation.5 | async-start | bytes 524288 | tf_op jit(solution)/shard_map/all_to_all | solution.py:132
  93.9 9.4 %all-to-all-start.6 = ((bf16[4,128,256]{1,2,0:T(8,128)(2,1)}), bf16[4,128,256]{1,2,0:T(8,128)(2,1)S(1)}, u32[]{:S(2)}, u32[]{:S(2)}) async-start(bf16[4,128,256]{1,2,0:T(8,128)(2,1)} %pad_maximum_fusion.1), calls=%async_computation.6 | async-start | bytes 524288 | tf_op jit(solution)/shard_map/all_to_all | solution.py:13
